TPU v7x, 32 devices: a whole 2x2x4 slice. The times are simulated.
32 devices in a mesh: seq: 8 (over z, x), head: 4 (over y, core).
Axes of the slice: x: 2, y: 2, z: 4, core: 2. Of those that a mesh axis runs over, the one named last changes fastest.
Arguments:
- queries: bfloat16 [768, 16384], P('head', 'seq'), may hold values from -10 to 10
- key_vectors: bfloat16 [768, 16384], P('head', 'seq'), may hold values from -4 to 4
- value_vectors: bfloat16 [768, 16384], P('head', 'seq'), may hold values from -6 to 6
- offsets: int32 [3, 12], replicated, may hold values from 0 to 15, as said below
- out_weight: bfloat16 [768, 768], replicated, may hold values from -0.75 to 0.75
Outputs:
- layer_out: bfloat16 [16384, 768], P(('seq', 'head'))
Inputs may be any that keep to these rules, and one draw needn't show every extreme that they name: offsets[0, h] < 4, offsets[1, h] < 16 and offsets[2, h] < 16; in each row some head has 0 and some head the largest allowed value.
All inputs are finite; a program needn't handle non-finite values.
Results may differ from a plain program's by a relative error of at most 0.0052.
Values may be sent and summed in bfloat16 or wider, within the bound.
No kernel may reach another device: no remote copies, remote signals or barrier semaphores. Data moves between devices by JAX's collectives and lax.ppermute only.
A program may use at most 128 MiB of HBM per device.

v0:
```python
import functools
import math

import jax
import jax.numpy as jnp
from jax import lax
from jax.experimental import pallas as pl
from jax.experimental.pallas import tpu as pltpu
from jax.sharding import PartitionSpec as P

DH = 64
KEYS = 1024
LANES = 128
QBLK = 256
EXP2_SCALE = DH ** (-0.5) * math.log2(math.e)
NT = (((1,), (1,)), ((), ()))
NN = (((1,), (0,)), ((), ()))
VMEM_BYTES = 48 << 20


def dot(a, b, dims):
    return lax.dot_general(a, b, dims, preferred_element_type=jnp.float32)


def lane_of(shape):
    return lax.broadcasted_iota(jnp.int32, shape, len(shape) - 1)


def softmax_block(scores):
    row_max = jnp.max(scores, axis=1, keepdims=True)
    weights = jnp.exp2((scores - row_max) * EXP2_SCALE).astype(jnp.bfloat16)
    return row_max, weights


def merge_rows(cur, cur_max, new, new_max):
    both = jnp.maximum(cur_max, new_max)
    keep_cur = jnp.exp2((cur_max - both) * EXP2_SCALE)
    keep_new = jnp.exp2((new_max - both) * EXP2_SCALE)
    return both, cur * keep_cur + new * keep_new


def select_kernel(dils, off_ref, q_ref, k_ref, v_ref, q1_ref, near_ref, far_ref, kvt, qt):
    heads = q_ref.shape[0] // DH
    tok = q_ref.shape[1]
    first = lax.axis_index("head") * heads
    n1 = tok // dils[0]
    for h in range(heads):
        rows = slice(h * DH, (h + 1) * DH)
        kvt[...] = jnp.concatenate([k_ref[rows, :], v_ref[rows, :]], 0).T.astype(jnp.float32)
        qt[...] = q_ref[rows, :].T.astype(jnp.float32)
        o1 = off_ref[0, first + h]
        q1_ref[h] = qt[pl.ds(o1, n1, stride=dils[0]), :].astype(jnp.bfloat16)
        near_ref[h, :n1, :] = kvt[pl.ds(o1, n1, stride=dils[0]), :].astype(jnp.bfloat16)
        q_parts = []
        for b in range(1, len(dils)):
            o = off_ref[b, first + h]
            n = tok // dils[b]
            q_parts.append(qt[pl.ds(o, n, stride=dils[b]), :])
            picked = kvt[pl.ds(o, n, stride=dils[b]), :]
            if b == 2:
                picked = pltpu.roll(picked, DH, 1)
            far_ref[b - 1, h] = picked.astype(jnp.bfloat16)
        if len(q_parts) == 1:
            q_parts.append(jnp.zeros_like(q_parts[0]))
        near_ref[h, n1:, :] = jnp.concatenate(q_parts, 1).astype(jnp.bfloat16)


def local_kernel(q_ref, k_ref, v_ref, acc_ref):
    tok = q_ref.shape[1]
    qt = q_ref[...].T
    for seg in range(tok // KEYS):
        cols = slice(seg * KEYS, (seg + 1) * KEYS)
        keys = k_ref[:, cols]
        vals = v_ref[:, cols]
        vals = jnp.concatenate([jnp.ones_like(vals), vals], 0)
        for blk in range(KEYS // QBLK):
            at = seg * KEYS + blk * QBLK
            row_max, weights = softmax_block(dot(qt[at : at + QBLK], keys, NN))
            out = dot(weights, vals, NT)
            acc_ref[0, at : at + QBLK, :] = jnp.where(lane_of(out.shape) == 0, row_max, out)


def pair_kernel(dil, off_ref, q_ref, own_ref, other_ref, acc_in, acc_ref):
    h = pl.program_id(0)
    heads = pl.num_programs(0)
    o = off_ref[0, lax.axis_index("head") * heads + h]
    n1 = q_ref.shape[1]
    acc_ref[...] = acc_in[...]
    kv = jnp.concatenate([own_ref[0, :n1, :], other_ref[0, :n1, :]], 0)
    keys = kv[:, :DH]
    vals = jnp.where(lane_of(kv.shape) < DH, jnp.ones_like(kv), kv)
    for blk in range(n1 // QBLK):
        rows = pl.ds(o + blk * QBLK * dil, QBLK, stride=dil)
        row_max, weights = softmax_block(dot(q_ref[0, blk * QBLK : (blk + 1) * QBLK], keys, NT))
        out = dot(weights, vals, NN)
        cur = acc_ref[0, rows, :]
        both, new = merge_rows(cur, cur[:, :1], out, row_max)
        acc_ref[0, rows, :] = jnp.where(lane_of(new.shape) == 0, both, new)


def far_kernel(branches, own_ref, other_ref, kv0, kv1, kv2, kv3, part_ref, send_ref):
    n1 = own_ref.shape[1] - LANES
    q_all = jnp.concatenate([own_ref[0, n1:, :], other_ref[0, n1:, :]], 0)
    lane_q = lane_of(q_all.shape)
    outs = []
    maxes = []
    for b in range(branches):
        kv = jnp.concatenate([r[b, 0] for r in (kv0, kv1, kv2, kv3)], 0)
        in_keys = (lane_of(kv.shape) < DH) == (b == 0)
        q_b = jnp.where((lane_q < DH) == (b == 0), q_all, jnp.zeros_like(q_all))
        row_max, weights = softmax_block(dot(q_b, kv, NT))
        vals = jnp.where(in_keys, jnp.ones_like(kv), kv)
        outs.append(dot(weights, vals, NN))
        maxes.append(row_max)
    n = q_all.shape[0] // 2
    lane = lane_of((n, LANES))
    for b in range(branches):
        part_ref[b, 0] = jnp.where(lane == (0 if b == 0 else LANES - 1), maxes[b][:n], outs[b][:n])
    out_a = outs[0][n:]
    out_b = outs[1][n:] if branches == 2 else out_a
    max_a = maxes[0][n:]
    max_b = maxes[1][n:] if branches == 2 else max_a
    send_ref[0, :n, :] = jnp.where(lane < DH, out_b, out_a).astype(jnp.bfloat16)
    sums = jnp.where(lane < DH, out_a, out_b)
    tops = jnp.where(lane < DH, max_a, max_b)
    slot = lane % DH
    stats = jnp.where(slot >= 3, sums, tops)
    high = stats.astype(jnp.bfloat16).astype(jnp.float32)
    mid = (stats - high).astype(jnp.bfloat16).astype(jnp.float32)
    low = stats - high - mid
    kind = slot % 3
    coded = jnp.where(kind == 0, high, jnp.where(kind == 1, mid, low))
    send_ref[0, n:, :] = coded.astype(jnp.bfloat16)


def finish_kernel(dils, off_ref, acc_in, part_ref, got_ref, o0, o1, o2, o3, acc):
    h = pl.program_id(0)
    heads = pl.num_programs(0)
    me = lax.axis_index("head")
    acc[...] = acc_in[0]
    n = part_ref.shape[2]
    got = got_ref[0, :n, :].astype(jnp.float32)
    coded = got_ref[0, n:, :].astype(jnp.float32)
    lane = lane_of((n, LANES))
    for b in range(len(dils)):
        o = off_ref[b + 1, me * heads + h]
        rows = pl.ds(o, n, stride=dils[b])
        cur = acc[rows, :]
        c = DH * b
        part = part_ref[b, 0]
        part_max = part[:, :1] if b == 0 else part[:, LANES - 1 :]
        got_max = coded[:, c : c + 1] + coded[:, c + 1 : c + 2] + coded[:, c + 2 : c + 3]
        got_sum = coded[:, c + 3 : c + 4] + coded[:, c + 4 : c + 5] + coded[:, c + 5 : c + 6]
        if b == 1:
            part = pltpu.roll(part, DH, 1)
            got_acc = pltpu.roll(got, DH, 1)
        else:
            got_acc = got
        new = jnp.where(lane < DH, got_sum, got_acc)
        part_max, part = merge_rows(part, part_max, new, got_max)
        both, cur = merge_rows(cur, cur[:, :1], part, part_max)
        acc[rows, :] = jnp.where(lane == 0, both, cur)
    flipped = acc[...].T
    done = (flipped[DH:, :] / flipped[1:2, :]).astype(jnp.bfloat16)
    outs = (o0, o1, o2, o3)
    width = o0.shape[1]
    for s, out in enumerate(outs):
        for dest in range(len(outs)):

            @pl.when((me ^ s) == dest)
            def _():
                out[...] = done[:, dest * width : (dest + 1) * width]


def project_kernel(x0, x1, x2, x3, w_ref, out_ref, xs):
    me = lax.axis_index("head")
    rows = x0.shape[0]
    for s, x in enumerate((x0, x1, x2, x3)):
        xs[pl.ds(pl.multiple_of((me ^ s) * rows, 64), rows), :] = x[...]
    out_ref[...] = dot(xs[...], w_ref[...], (((0,), (0,)), ((), ()))).astype(jnp.bfloat16)


def partner(block, axis, apart):
    count = lax.axis_size(axis)
    return lax.ppermute(block, axis, [(i, i ^ apart) for i in range(count)])


def params():
    return pltpu.CompilerParams(vmem_limit_bytes=VMEM_BYTES)


def whole():
    return pl.BlockSpec(memory_space=pltpu.VMEM)


def smem():
    return pl.BlockSpec(memory_space=pltpu.SMEM)


def by_head(shape):
    return pl.BlockSpec((1,) + shape, lambda h: (h, 0, 0))


def cost(queries, keys):
    return pl.CostEstimate(
        flops=queries * keys * 512, bytes_accessed=queries * 2048, transcendentals=queries * keys
    )


def spread_far(acc, query_h, key_h, value_h, dil, head_offsets):
    hit = jnp.arange(dil)[None, :] == head_offsets[:, None]

    def pick(x):
        shaped = x.reshape(x.shape[:2] + (x.shape[2] // dil, dil))
        return jnp.sum(shaped * hit[:, None, None, :].astype(x.dtype), axis=-1, dtype=x.dtype)

    pair = lax.all_gather(jnp.stack([pick(key_h), pick(value_h)], 0), "seq", axis=3, tiled=True)
    scores = jnp.einsum("hdq,hdk->hqk", pick(query_h), pair[0], preferred_element_type=jnp.float32)
    new_max = jnp.max(scores, axis=2)
    e = jnp.exp2((scores - new_max[:, :, None]) * EXP2_SCALE)
    new_sum = jnp.sum(e, axis=2)
    new_acc = jnp.einsum(
        "hqk,hdk->hqd", e.astype(jnp.bfloat16), pair[1], preferred_element_type=jnp.float32
    )
    heads, tok, _ = acc.shape
    shaped = acc.reshape(heads, tok // dil, dil, LANES)
    cur = jnp.sum(jnp.where(hit[:, None, :, None], shaped, 0.0), axis=2)
    new = jnp.concatenate([jnp.broadcast_to(new_sum[:, :, None], new_acc.shape), new_acc], 2)
    both, out = merge_rows(cur, cur[:, :, :1], new, new_max[:, :, None])
    out = jnp.where(jnp.arange(LANES) == 0, both, out)
    return jnp.where(hit[:, None, :, None], out[:, :, None, :], shaped).reshape(acc.shape)


def local(queries, key_vectors, value_vectors, offsets, out_weight):
    tok = queries.shape[1]
    heads = queries.shape[0] // DH
    seq_count = lax.axis_size("seq")
    far_rate = tok * seq_count // KEYS
    dils = (4, 16, far_rate) if far_rate == 16 else (4, 16)
    branches = len(dils) - 1
    n1, n2 = tok // 4, tok // 16
    bf16, f32 = jnp.bfloat16, jnp.float32
    struct = jax.ShapeDtypeStruct

    q1, near, far = pl.pallas_call(
        functools.partial(select_kernel, dils),
        out_shape=(
            struct((heads, n1, DH), bf16),
            struct((heads, n1 + n2, LANES), bf16),
            struct((branches, heads, n2, LANES), bf16),
        ),
        in_specs=[smem(), whole(), whole(), whole()],
        out_specs=(whole(), whole(), whole()),
        scratch_shapes=[pltpu.VMEM((tok, LANES), f32), pltpu.VMEM((tok, DH), f32)],
        compiler_params=params(),
        name="select",
    )(offsets, queries, key_vectors, value_vectors)

    fars = [far] + [partner(far, "seq", apart) for apart in (2, 4, 6)]
    near_other = partner(near, "seq", 1)

    by_rows = pl.BlockSpec((DH, tok), lambda h: (h, 0))
    acc = pl.pallas_call(
        local_kernel,
        grid=(heads,),
        out_shape=struct((heads, tok, LANES), f32),
        in_specs=[by_rows, by_rows, by_rows],
        out_specs=by_head((tok, LANES)),
        compiler_params=params(),
        cost_estimate=cost(heads * tok, KEYS),
        name="local",
    )(queries, key_vectors, value_vectors)

    acc = pl.pallas_call(
        functools.partial(pair_kernel, 4),
        grid=(heads,),
        out_shape=struct((heads, tok, LANES), f32),
        in_specs=[smem(), by_head((n1, DH)), by_head((n1 + n2, LANES)), by_head((n1 + n2, LANES)), by_head((tok, LANES))],
        out_specs=by_head((tok, LANES)),
        input_output_aliases={4: 0},
        compiler_params=params(),
        cost_estimate=cost(heads * n1, KEYS),
        name="pair",
    )(offsets, q1, near, near_other, acc)

    if branches == 1:
        shape = (heads, DH, tok)
        my_offsets = lax.dynamic_slice_in_dim(offsets[2], lax.axis_index("head") * heads, heads, 0)
        acc = spread_far(
            acc, queries.reshape(shape), key_vectors.reshape(shape), value_vectors.reshape(shape), far_rate, my_offsets
        )

    far_spec = pl.BlockSpec((branches, 1, n2, LANES), lambda h: (0, h, 0, 0))
    part, send = pl.pallas_call(
        functools.partial(far_kernel, branches),
        grid=(heads,),
        out_shape=(struct((branches, heads, n2, LANES), f32), struct((heads, 2 * n2, LANES), bf16)),
        in_specs=[by_head((n1 + n2, LANES))] * 2 + [far_spec] * 4,
        out_specs=(far_spec, by_head((2 * n2, LANES))),
        compiler_params=params(),
        cost_estimate=cost(heads * n2 * 4, KEYS // 2),
        name="far",
    )(near, near_other, *fars)
    got = partner(send, "seq", 1)

    head_count = lax.axis_size("head")
    width = tok // head_count
    out_spec = pl.BlockSpec((DH, width), lambda h: (h, 0))
    blocks = pl.pallas_call(
        functools.partial(finish_kernel, dils[1:]),
        grid=(heads,),
        out_shape=(struct((heads * DH, width), bf16),) * head_count,
        in_specs=[smem(), by_head((tok, LANES)), far_spec, by_head((2 * n2, LANES))],
        out_specs=(out_spec,) * head_count,
        scratch_shapes=[pltpu.VMEM((tok, LANES), f32)],
        compiler_params=params(),
        name="finish",
    )(offsets, acc, part, got)

    landed = [blocks[0]] + [partner(blocks[s], "head", s) for s in range(1, head_count)]
    return pl.pallas_call(
        project_kernel,
        out_shape=struct((width, out_weight.shape[1]), bf16),
        in_specs=[whole()] * (head_count + 1),
        out_specs=whole(),
        scratch_shapes=[pltpu.VMEM((head_count * heads * DH, width), bf16)],
        compiler_params=params(),
        name="project",
    )(*landed, out_weight)


def solution(mesh):
    in_specs = (P("head", "seq"), P("head", "seq"), P("head", "seq"), P(), P())
    out_specs = P(("seq", "head"), None)
    return jax.shard_map(local, mesh=mesh, in_specs=in_specs, out_specs=out_specs, check_vma=False)
```

profile of v0, /device:TPU:0, one launch (start us, length us, event | category | flops | bytes accessed | tf_op | source)
XLA Modules:
  0.0 61.0 jit_solution(13157435994969092794)
XLA Ops:
  0.0 1.1 %copy-done.1 = bf16[192,2048]{1,0:T(8,128)(2,1)S(1)} copy-done((bf16[192,2048]{1,0:T(8,128)(2,1)S(1)}, bf16[192,2048]{1,0:T(8,128)(2,1)}, u32[]{:S(2)}) %copy-start.1) | copy-done | bytes 786456
  1.1 1.1 %copy-done.3 = bf16[192,2048]{1,0:T(8,128)(2,1)S(1)} copy-done((bf16[192,2048]{1,0:T(8,128)(2,1)S(1)}, bf16[192,2048]{1,0:T(8,128)(2,1)}, u32[]{:S(2)}) %copy-start.3) | copy-done | bytes 786456
  2.3 1.1 %copy-done.5 = bf16[192,2048]{1,0:T(8,128)(2,1)S(1)} copy-done((bf16[192,2048]{1,0:T(8,128)(2,1)S(1)}, bf16[192,2048]{1,0:T(8,128)(2,1)}, u32[]{:S(2)}) %copy-start.5) | copy-done | bytes 786456
  3.4 0.7 %copy-done.7 = s32[3,12]{1,0:T(4,128)S(1)} copy-done((s32[3,12]{1,0:T(4,128)S(1)}, s32[3,12]{1,0:T(4,128)}, u32[]{:S(2)}) %copy-start.7) | copy-done | bytes 168
  4.1 1.9 %select.1 = (bf16[3,512,64]{2,1,0:T(8,128)(2,1)S(1)}, bf16[3,640,128]{2,1,0:T(8,128)(2,1)S(1)}, bf16[2,3,128,128]{3,2,1,0:T(8,128)(2,1)S(1)}) custom-call(s32[3,12]{1,0:T(4,128)S(1)} %copy-done.7, bf16[192,2048]{1,0:T(8,128)(2,1)S(1)} %copy-done.1, bf16[192,2048]{1,0:T(8,128)(2,1)S(1)} %copy-done.3, bf16[192,2048]{1,0:T(8,128)(2,1)S(1)} %copy-done.5), custom_call_target="tpu_custom_call" | custom-call | tf_op jit(solution)/shard_map/select/pallas_call | solution.py:245
  6.0 3.0 %collective-permute-start = (bf16[3,640,128]{2,1,0:T(8,128)(2,1)S(1)}, bf16[3,640,128]{2,1,0:T(8,128)(2,1)S(1)}, u32[]{:S(2)}, u32[]{:S(2)}) collective-permute-start(bf16[3,640,128]{2,1,0:T(8,128)(2,1)S(1)} %get-tuple-element.15.own_ref), channel_id=1, source_target_pairs={{0,4},{4,0},{8,12},{12,8},{16,20},{20,16},{24,28},{28,24},{1,5},{5... | collective-permute-start | bytes 1474568 | tf_op jit(solution)/shard_map/ppermute | solution.py:185
  9.0 1.6 %collective-permute-start.1 = (bf16[2,3,128,128]{3,2,1,0:T(8,128)(2,1)S(1)}, bf16[2,3,128,128]{3,2,1,0:T(8,128)(2,1)S(1)}, u32[]{:S(2)}, u32[]{:S(2)}) collective-permute-start(bf16[2,3,128,128]{3,2,1,0:T(8,128)(2,1)S(1)} %get-tuple-element.16.kv0), channel_id=1, source_target_pairs={{0,8},{4,12},{8,0},{12,4},{16,24},{20,28},{24,16},{28,20},{1,9},{5... | collective-permute-start | bytes 589832 | tf_op jit(solution)/shard_map/ppermute | solution.py:185
  10.6 2.6 %collective-permute-start.2 = (bf16[2,3,128,128]{3,2,1,0:T(8,128)(2,1)S(1)}, bf16[2,3,128,128]{3,2,1,0:T(8,128)(2,1)S(1)}, u32[]{:S(2)}, u32[]{:S(2)}) collective-permute-start(bf16[2,3,128,128]{3,2,1,0:T(8,128)(2,1)S(1)} %get-tuple-element.16.kv0), channel_id=1, source_target_pairs={{0,16},{4,20},{8,24},{12,28},{16,0},{20,4},{24,8},{28,12},{1,17},{... | collective-permute-start | bytes 589832 | tf_op jit(solution)/shard_map/ppermute | solution.py:185
  13.2 0.2 collective-permute-start.3
  13.4 5.1 %collective-permute-done.1.kv1 = bf16[2,3,128,128]{3,2,1,0:T(8,128)(2,1)S(1)} collective-permute-done((bf16[2,3,128,128]{3,2,1,0:T(8,128)(2,1)S(1)}, bf16[2,3,128,128]{3,2,1,0:T(8,128)(2,1)S(1)}, u32[]{:S(2)}, u32[]{:S(2)}) %collective-permute-start.1) | collective-permute-done | bytes 196640 | tf_op jit(solution)/shard_map/ppermute | solution.py:185
  18.5 9.2 %collective-permute-done.2.kv2 = bf16[2,3,128,128]{3,2,1,0:T(8,128)(2,1)S(1)} collective-permute-done((bf16[2,3,128,128]{3,2,1,0:T(8,128)(2,1)S(1)}, bf16[2,3,128,128]{3,2,1,0:T(8,128)(2,1)S(1)}, u32[]{:S(2)}, u32[]{:S(2)}) %collective-permute-start.2) | collective-permute-done | bytes 196640 | tf_op jit(solution)/shard_map/ppermute | solution.py:185
  27.7 0.0 collective-permute-done.3.kv3
  27.7 2.4 %far.1 = (f32[2,3,128,128]{3,2,1,0:T(8,128)S(1)}, bf16[3,256,128]{2,1,0:T(8,128)(2,1)S(1)}) custom-call(bf16[3,640,128]{2,1,0:T(8,128)(2,1)S(1)} %get-tuple-element.15.own_ref, bf16[3,640,128]{2,1,0:T(8,128)(2,1)S(1)} %collective-permute-done.other_ref, bf16[2,3,128,128]{3,2,1,0:T(8,128)(2,1)S(1)} %get-tuple-element.16.kv0, ...), custom_call_target="tpu_custom_call" | custom-call | flops 402653184 | bytes 3145728 | tf_op jit(solution)/shard_map/far/pallas_call | solution.py:294
  30.2 0.6 collective-permute-start.4
  30.8 9.1 %local.1.acc_in = f32[3,2048,128]{2,1,0:T(8,128)S(1)} custom-call(bf16[192,2048]{1,0:T(8,128)(2,1)S(1)} %copy-done.2, bf16[192,2048]{1,0:T(8,128)(2,1)S(1)} %copy-done.4, bf16[192,2048]{1,0:T(8,128)(2,1)S(1)} %copy-done.6), custom_call_target="tpu_custom_call" | custom-call | flops 3221225472 | bytes 12582912 | tf_op jit(solution)/shard_map/local/pallas_call | solution.py:263
  39.9 4.2 %pair.1.acc_in = f32[3,2048,128]{2,1,0:T(8,128)S(1)} custom-call(s32[3,12]{1,0:T(4,128)S(1)} %copy-done.7, bf16[3,512,64]{2,1,0:T(8,128)(2,1)S(1)} %get-tuple-element.14.q_ref, bf16[3,640,128]{2,1,0:T(8,128)(2,1)S(1)} %get-tuple-element.15.own_ref, bf16[3,640,128]{2,1,0:T(8,128)(2,1)S(1)} %collective-permute-done.other_ref, ...), custom_call_target="tpu_custom_call", output_to_operand_aliasing={{}: (4, {})} | custom-call | flops 805306368 | bytes 3145728 | tf_op jit(solution)/shard_map/pair/pallas_call | solution.py:274
  44.1 0.0 copy-start
  44.1 4.0 %finish.1 = (bf16[192,512]{1,0:T(8,128)(2,1)S(1)}, bf16[192,512]{1,0:T(8,128)(2,1)S(1)}, bf16[192,512]{1,0:T(8,128)(2,1)S(1)}, bf16[192,512]{1,0:T(8,128)(2,1)S(1)}) custom-call(s32[3,12]{1,0:T(4,128)S(1)} %copy-done.7, f32[3,2048,128]{2,1,0:T(8,128)S(1)} %pair.1.acc_in, f32[2,3,128,128]{3,2,1,0:T(8,128)S(1)} %get-tuple-element.17.part_ref, ...), custom_call_target="tpu_custom_call" | custom-call | tf_op jit(solution)/shard_map/finish/pallas_call | solution.py:309
  48.1 0.1 collective-permute-start.5
  48.2 1.6 %collective-permute-start.6 = (bf16[192,512]{1,0:T(8,128)(2,1)S(1)}, bf16[192,512]{1,0:T(8,128)(2,1)S(1)}, u32[]{:S(2)}, u32[]{:S(2)}) collective-permute-start(bf16[192,512]{1,0:T(8,128)(2,1)S(1)} %get-tuple-element.21), channel_id=1, source_target_pairs={{0,2},{1,3},{2,0},{3,1},{4,6},{5,7},{6,4},{7,5},{8,10},{9,11},{10,... | collective-permute-start | bytes 589832 | tf_op jit(solution)/shard_map/ppermute | solution.py:185
  49.7 0.3 collective-permute-start.7
  50.0 5.9 %collective-permute-done.6.x2 = bf16[192,512]{1,0:T(8,128)(2,1)S(1)} collective-permute-done((bf16[192,512]{1,0:T(8,128)(2,1)S(1)}, bf16[192,512]{1,0:T(8,128)(2,1)S(1)}, u32[]{:S(2)}, u32[]{:S(2)}) %collective-permute-start.6) | collective-permute-done | bytes 196640 | tf_op jit(solution)/shard_map/ppermute | solution.py:185
  56.0 3.3 %collective-permute-done.7.x3 = bf16[192,512]{1,0:T(8,128)(2,1)S(1)} collective-permute-done((bf16[192,512]{1,0:T(8,128)(2,1)S(1)}, bf16[192,512]{1,0:T(8,128)(2,1)S(1)}, u32[]{:S(2)}, u32[]{:S(2)}) %collective-permute-start.7) | collective-permute-done | bytes 196640 | tf_op jit(solution)/shard_map/ppermute | solution.py:185
  59.3 1.8 %project.1 = bf16[512,768]{1,0:T(8,128)(2,1)} custom-call(bf16[192,512]{1,0:T(8,128)(2,1)S(1)} %get-tuple-element.19.x0, bf16[192,512]{1,0:T(8,128)(2,1)S(1)} %collective-permute-done.5.x1, bf16[192,512]{1,0:T(8,128)(2,1)S(1)} %collective-permute-done.6.x2, bf16[192,512]{1,0:T(8,128)(2,1)S(1)} %collective-permute-done.7.x3, bf16[768,768]{1,0:T(8,128)(2,1)S(1)} %copy-done), custom_call_target="tpu_custom_call" | custom-call | tf_op jit(solution)/shard_map/project/pallas_call | solution.py:321
  (14 shorter events, 0.0 us)
Async XLA Ops:
  0.0 1.1 %copy-start.1 = (bf16[192,2048]{1,0:T(8,128)(2,1)S(1)}, bf16[192,2048]{1,0:T(8,128)(2,1)}, u32[]{:S(2)}) copy-start(bf16[192,2048]{1,0:T(8,128)(2,1)} %q_ref.3) | copy-start | bytes 2359300
  1.1 1.1 %copy-start.3 = (bf16[192,2048]{1,0:T(8,128)(2,1)S(1)}, bf16[192,2048]{1,0:T(8,128)(2,1)}, u32[]{:S(2)}) copy-start(bf16[192,2048]{1,0:T(8,128)(2,1)} %k_ref.3) | copy-start | bytes 2359300
  2.3 1.1 %copy-start.5 = (bf16[192,2048]{1,0:T(8,128)(2,1)S(1)}, bf16[192,2048]{1,0:T(8,128)(2,1)}, u32[]{:S(2)}) copy-start(bf16[192,2048]{1,0:T(8,128)(2,1)} %v_ref.3) | copy-start | bytes 2359300
  3.4 0.7 %copy-start.7 = (s32[3,12]{1,0:T(4,128)S(1)}, s32[3,12]{1,0:T(4,128)}, u32[]{:S(2)}) copy-start(s32[3,12]{1,0:T(4,128)} %off_ref.5) | copy-start | bytes 436
  4.1 26.7 %copy-start.2 = (bf16[192,2048]{1,0:T(8,128)(2,1)S(1)}, bf16[192,2048]{1,0:T(8,128)(2,1)}, u32[]{:S(2)}) copy-start(bf16[192,2048]{1,0:T(8,128)(2,1)} %q_ref.3) | copy-start | bytes 2359300
  4.1 26.7 %copy-start.4 = (bf16[192,2048]{1,0:T(8,128)(2,1)S(1)}, bf16[192,2048]{1,0:T(8,128)(2,1)}, u32[]{:S(2)}) copy-start(bf16[192,2048]{1,0:T(8,128)(2,1)} %k_ref.3) | copy-start | bytes 2359300
  4.1 26.7 %copy-start.6 = (bf16[192,2048]{1,0:T(8,128)(2,1)S(1)}, bf16[192,2048]{1,0:T(8,128)(2,1)}, u32[]{:S(2)}) copy-start(bf16[192,2048]{1,0:T(8,128)(2,1)} %v_ref.3) | copy-start | bytes 2359300
  6.0 21.8 %collective-permute-start = (bf16[3,640,128]{2,1,0:T(8,128)(2,1)S(1)}, bf16[3,640,128]{2,1,0:T(8,128)(2,1)S(1)}, u32[]{:S(2)}, u32[]{:S(2)}) collective-permute-start(bf16[3,640,128]{2,1,0:T(8,128)(2,1)S(1)} %get-tuple-element.15.own_ref), channel_id=1, source_target_pairs={{0,4},{4,0},{8,12},{12,8},{16,20},{20,16},{24,28},{28,24},{1,5},{5... | collective-permute-start | bytes 1474568 | tf_op jit(solution)/shard_map/ppermute | solution.py:185
  9.0 9.5 %collective-permute-start.1 = (bf16[2,3,128,128]{3,2,1,0:T(8,128)(2,1)S(1)}, bf16[2,3,128,128]{3,2,1,0:T(8,128)(2,1)S(1)}, u32[]{:S(2)}, u32[]{:S(2)}) collective-permute-start(bf16[2,3,128,128]{3,2,1,0:T(8,128)(2,1)S(1)} %get-tuple-element.16.kv0), channel_id=1, source_target_pairs={{0,8},{4,12},{8,0},{12,4},{16,24},{20,28},{24,16},{28,20},{1,9},{5... | collective-permute-start | bytes 589832 | tf_op jit(solution)/shard_map/ppermute | solution.py:185
  10.6 17.2 %collective-permute-start.2 = (bf16[2,3,128,128]{3,2,1,0:T(8,128)(2,1)S(1)}, bf16[2,3,128,128]{3,2,1,0:T(8,128)(2,1)S(1)}, u32[]{:S(2)}, u32[]{:S(2)}) collective-permute-start(bf16[2,3,128,128]{3,2,1,0:T(8,128)(2,1)S(1)} %get-tuple-element.16.kv0), channel_id=1, source_target_pairs={{0,16},{4,20},{8,24},{12,28},{16,0},{20,4},{24,8},{28,12},{1,17},{... | collective-permute-start | bytes 589832 | tf_op jit(solution)/shard_map/ppermute | solution.py:185
  13.2 14.6 %collective-permute-start.3 = (bf16[2,3,128,128]{3,2,1,0:T(8,128)(2,1)S(1)}, bf16[2,3,128,128]{3,2,1,0:T(8,128)(2,1)S(1)}, u32[]{:S(2)}, u32[]{:S(2)}) collective-permute-start(bf16[2,3,128,128]{3,2,1,0:T(8,128)(2,1)S(1)} %get-tuple-element.16.kv0), channel_id=1, source_target_pairs={{0,24},{4,28},{8,16},{12,20},{16,8},{20,12},{24,0},{28,4},{1,25},{... | collective-permute-start | bytes 589832 | tf_op jit(solution)/shard_map/ppermute | solution.py:185
  30.2 13.9 %collective-permute-start.4 = (bf16[3,256,128]{2,1,0:T(8,128)(2,1)S(1)}, bf16[3,256,128]{2,1,0:T(8,128)(2,1)S(1)}, u32[]{:S(2)}, u32[]{:S(2)}) collective-permute-start(bf16[3,256,128]{2,1,0:T(8,128)(2,1)S(1)} %get-tuple-element.18), channel_id=1, source_target_pairs={{0,4},{4,0},{8,12},{12,8},{16,20},{20,16},{24,28},{28,24},{1,5},{5... | collective-permute-start | bytes 589832 | tf_op jit(solution)/shard_map/ppermute | solution.py:185
  44.1 15.2 %copy-start = (bf16[768,768]{1,0:T(8,128)(2,1)S(1)}, bf16[768,768]{1,0:T(8,128)(2,1)}, u32[]{:S(2)}) copy-start(bf16[768,768]{1,0:T(8,128)(2,1)} %w_ref.1) | copy-start | bytes 3538948
  48.1 1.9 %collective-permute-start.5 = (bf16[192,512]{1,0:T(8,128)(2,1)S(1)}, bf16[192,512]{1,0:T(8,128)(2,1)S(1)}, u32[]{:S(2)}, u32[]{:S(2)}) collective-permute-start(bf16[192,512]{1,0:T(8,128)(2,1)S(1)} %get-tuple-element.20), channel_id=1, source_target_pairs={{0,1},{1,0},{2,3},{3,2},{4,5},{5,4},{6,7},{7,6},{8,9},{9,8},{10,11... | collective-permute-start | bytes 589832 | tf_op jit(solution)/shard_map/ppermute | solution.py:185
  48.2 7.8 %collective-permute-start.6 = (bf16[192,512]{1,0:T(8,128)(2,1)S(1)}, bf16[192,512]{1,0:T(8,128)(2,1)S(1)}, u32[]{:S(2)}, u32[]{:S(2)}) collective-permute-start(bf16[192,512]{1,0:T(8,128)(2,1)S(1)} %get-tuple-element.21), channel_id=1, source_target_pairs={{0,2},{1,3},{2,0},{3,1},{4,6},{5,7},{6,4},{7,5},{8,10},{9,11},{10,... | collective-permute-start | bytes 589832 | tf_op jit(solution)/shard_map/ppermute | solution.py:185
  49.7 9.5 %collective-permute-start.7 = (bf16[192,512]{1,0:T(8,128)(2,1)S(1)}, bf16[192,512]{1,0:T(8,128)(2,1)S(1)}, u32[]{:S(2)}, u32[]{:S(2)}) collective-permute-start(bf16[192,512]{1,0:T(8,128)(2,1)S(1)} %get-tuple-element.22), channel_id=1, source_target_pairs={{0,3},{1,2},{2,1},{3,0},{4,7},{5,6},{6,5},{7,4},{8,11},{9,10},{10,... | collective-permute-start | bytes 589832 | tf_op jit(solution)/shard_map/ppermute | solution.py:185
where the time goes:
time: 61.8 us; the launch traced here: 61 us
  waiting for transfers between devices  23.6 us (38%)
  Pallas kernels  23.4 us (38%)
  starting transfers between devices  9.91 us (16%)
  local copies, waits for them, and re-layouts  4.1 us (7%)
    ppermute x8, waiting for transfers between devices, partner(): return lax.ppermute(block, axis, [(i, i ^ apart) for i in range(count)])  23.6 us
    ppermute x8, starting transfers between devices, partner(): return lax.ppermute(block, axis, [(i, i ^ apart) for i in range(count)])  9.91 us
    pallas_call x1, Pallas kernels, local(): pl.pallas_call(local_kernel, grid=(heads,), out_shape=struct((heads, tok,...  9.09 us
    pallas_call x1, Pallas kernels, local(): pl.pallas_call(functools.partial(pair_kernel, 4), grid=(heads,), out_shap...  4.19 us
    unnamed x16, local copies, waits for them, and re-layouts  4.1 us
    pallas_call x1, Pallas kernels, local(): pl.pallas_call(functools.partial(finish_kernel, dils[1:]), grid=(heads,),...  4 us
    pallas_call x1, Pallas kernels, local(): pl.pallas_call(functools.partial(far_kernel, branches), grid=(heads,), ou...  2.44 us
    pallas_call x1, Pallas kernels, local(): pl.pallas_call(functools.partial(select_kernel, dils), out_shape=(struct(...  1.9 us
  transfers between devices with their start and end apart: 8, of which 4 were waited for; matrix products, arithmetic and copies ran while one was open for 0% of the time, Pallas kernels for 22%

commit v1 on v0

--- a/solution.py
+++ b/solution.py
@@ -40,29 +40,26 @@
 
 
 def select_kernel(dils, off_ref, q_ref, k_ref, v_ref, q1_ref, near_ref, far_ref, kvt, qt):
-    heads = q_ref.shape[0] // DH
     tok = q_ref.shape[1]
-    first = lax.axis_index("head") * heads
+    head = lax.axis_index("head") * pl.num_programs(0) + pl.program_id(0)
     n1 = tok // dils[0]
-    for h in range(heads):
-        rows = slice(h * DH, (h + 1) * DH)
-        kvt[...] = jnp.concatenate([k_ref[rows, :], v_ref[rows, :]], 0).T.astype(jnp.float32)
-        qt[...] = q_ref[rows, :].T.astype(jnp.float32)
-        o1 = off_ref[0, first + h]
-        q1_ref[h] = qt[pl.ds(o1, n1, stride=dils[0]), :].astype(jnp.bfloat16)
-        near_ref[h, :n1, :] = kvt[pl.ds(o1, n1, stride=dils[0]), :].astype(jnp.bfloat16)
-        q_parts = []
-        for b in range(1, len(dils)):
-            o = off_ref[b, first + h]
-            n = tok // dils[b]
-            q_parts.append(qt[pl.ds(o, n, stride=dils[b]), :])
-            picked = kvt[pl.ds(o, n, stride=dils[b]), :]
-            if b == 2:
-                picked = pltpu.roll(picked, DH, 1)
-            far_ref[b - 1, h] = picked.astype(jnp.bfloat16)
-        if len(q_parts) == 1:
-            q_parts.append(jnp.zeros_like(q_parts[0]))
-        near_ref[h, n1:, :] = jnp.concatenate(q_parts, 1).astype(jnp.bfloat16)
+    kvt[...] = jnp.concatenate([k_ref[...], v_ref[...]], 0).T.astype(jnp.float32)
+    qt[...] = q_ref[...].T.astype(jnp.float32)
+    o1 = off_ref[0, head]
+    q1_ref[0] = qt[pl.ds(o1, n1, stride=dils[0]), :].astype(jnp.bfloat16)
+    near_ref[0, :n1, :] = kvt[pl.ds(o1, n1, stride=dils[0]), :].astype(jnp.bfloat16)
+    q_parts = []
+    for b in range(1, len(dils)):
+        o = off_ref[b, head]
+        n = tok // dils[b]
+        q_parts.append(qt[pl.ds(o, n, stride=dils[b]), :])
+        picked = kvt[pl.ds(o, n, stride=dils[b]), :]
+        if b == 2:
+            picked = pltpu.roll(picked, DH, 1)
+        far_ref[b - 1, 0] = picked.astype(jnp.bfloat16)
+    if len(q_parts) == 1:
+        q_parts.append(jnp.zeros_like(q_parts[0]))
+    near_ref[0, n1:, :] = jnp.concatenate(q_parts, 1).astype(jnp.bfloat16)
 
 
 def local_kernel(q_ref, k_ref, v_ref, acc_ref):
@@ -185,8 +182,8 @@
     return lax.ppermute(block, axis, [(i, i ^ apart) for i in range(count)])
 
 
-def params():
-    return pltpu.CompilerParams(vmem_limit_bytes=VMEM_BYTES)
+def params(limit=None):
+    return pltpu.CompilerParams(vmem_limit_bytes=limit)
 
 
 def whole():
@@ -242,6 +239,8 @@
     bf16, f32 = jnp.bfloat16, jnp.float32
     struct = jax.ShapeDtypeStruct
 
+    by_rows = pl.BlockSpec((DH, tok), lambda h: (h, 0))
+    far_spec = pl.BlockSpec((branches, 1, n2, LANES), lambda h: (0, h, 0, 0))
     q1, near, far = pl.pallas_call(
         functools.partial(select_kernel, dils),
         out_shape=(
@@ -249,8 +248,9 @@
             struct((heads, n1 + n2, LANES), bf16),
             struct((branches, heads, n2, LANES), bf16),
         ),
-        in_specs=[smem(), whole(), whole(), whole()],
-        out_specs=(whole(), whole(), whole()),
+        grid=(heads,),
+        in_specs=[smem(), by_rows, by_rows, by_rows],
+        out_specs=(by_head((n1, DH)), by_head((n1 + n2, LANES)), far_spec),
         scratch_shapes=[pltpu.VMEM((tok, LANES), f32), pltpu.VMEM((tok, DH), f32)],
         compiler_params=params(),
         name="select",
@@ -259,7 +259,6 @@
     fars = [far] + [partner(far, "seq", apart) for apart in (2, 4, 6)]
     near_other = partner(near, "seq", 1)
 
-    by_rows = pl.BlockSpec((DH, tok), lambda h: (h, 0))
     acc = pl.pallas_call(
         local_kernel,
         grid=(heads,),
@@ -290,7 +289,7 @@
             acc, queries.reshape(shape), key_vectors.reshape(shape), value_vectors.reshape(shape), far_rate, my_offsets
         )
 
-    far_spec = pl.BlockSpec((branches, 1, n2, LANES), lambda h: (0, h, 0, 0))
+    fars, acc = lax.optimization_barrier((fars, acc))
     part, send = pl.pallas_call(
         functools.partial(far_kernel, branches),
         grid=(heads,),
@@ -324,7 +323,7 @@
         in_specs=[whole()] * (head_count + 1),
         out_specs=whole(),
         scratch_shapes=[pltpu.VMEM((head_count * heads * DH, width), bf16)],
-        compiler_params=params(),
+        compiler_params=params(VMEM_BYTES),
         name="project",
     )(*landed, out_weight)
 

time: 61.8 us -> 62.2 us (level)
  Pallas kernels: 23.4 us -> 33.4 us
  waiting for transfers between devices: 23.6 us -> 15 us
    ppermute x8, waiting for transfers between devices: 23.6 us -> 15 us  [partner(): return lax.ppermute(block, axis, [(i, i ^ apart) for i in range(count)])]
    pallas_call x1, Pallas kernels: 4.19 us -> 6.53 us  [local(): pl.pallas_call(functools.partial(pair_kernel, 4), grid=(heads,), out_shap...]
    pallas_call x1, Pallas kernels: 1.9 us -> 3.99 us  [local(): pl.pallas_call(functools.partial(select_kernel, dils), out_shape=(struct(...]
    pallas_call x1, Pallas kernels: 9.09 us -> 11.1 us  [local(): pl.pallas_call(local_kernel, grid=(heads,), out_shape=struct((heads, tok,...]
    pallas_call x1, Pallas kernels: 2.44 us -> 4.49 us  [local(): pl.pallas_call(functools.partial(far_kernel, branches), grid=(heads,), ou...]
    pallas_call x1, Pallas kernels: 4 us -> 5.5 us  [local(): pl.pallas_call(functools.partial(finish_kernel, dils[1:]), grid=(heads,),...]
    unnamed x16 -> x14, local copies, waits for them, and re-layouts: 4.1 us -> 3.8 us
  transfers between devices with their start and end apart: 8 -> 8, of which waited for: 4 -> 3; matrix products, arithmetic and copies ran while one was open for 0% -> 0% of each run, Pallas kernels for 22% -> 29%
where the time goes in v1:
time: 62.2 us; the launch traced here: 61.8 us
  Pallas kernels  33.4 us (54%)
  waiting for transfers between devices  15 us (24%)
  starting transfers between devices  9.53 us (15%)
  local copies, waits for them, and re-layouts  3.8 us (6%)
    ppermute x8, waiting for transfers between devices, partner(): return lax.ppermute(block, axis, [(i, i ^ apart) for i in range(count)])  15 us
    pallas_call x1, Pallas kernels, local(): pl.pallas_call(local_kernel, grid=(heads,), out_shape=struct((heads, tok,...  11.1 us
    ppermute x8, starting transfers between devices, partner(): return lax.ppermute(block, axis, [(i, i ^ apart) for i in range(count)])  9.53 us
    pallas_call x1, Pallas kernels, local(): pl.pallas_call(functools.partial(pair_kernel, 4), grid=(heads,), out_shap...  6.53 us
    pallas_call x1, Pallas kernels, local(): pl.pallas_call(functools.partial(finish_kernel, dils[1:]), grid=(heads,),...  5.5 us
    pallas_call x1, Pallas kernels, local(): pl.pallas_call(functools.partial(far_kernel, branches), grid=(heads,), ou...  4.49 us
    pallas_call x1, Pallas kernels, local(): pl.pallas_call(functools.partial(select_kernel, dils), out_shape=(struct(...  3.99 us
    unnamed x14, local copies, waits for them, and re-layouts  3.8 us
  transfers between devices with their start and end apart: 8, of which 3 were waited for; matrix products, arithmetic and copies ran while one was open for 0% of the time, Pallas kernels for 29%

profile of v1, /device:TPU:0, one launch (start us, length us, event | category | flops | bytes accessed | tf_op | source)
XLA Modules:
  0.0 61.8 jit_solution(6175264460843625258)
XLA Ops:
  0.0 4.0 %select.1 = (bf16[3,512,64]{2,1,0:T(8,128)(2,1)}, bf16[3,640,128]{2,1,0:T(8,128)(2,1)}, bf16[2,3,128,128]{3,2,1,0:T(8,128)(2,1)}) custom-call(s32[3,12]{1,0:T(4,128)} %off_ref.5, bf16[192,2048]{1,0:T(8,128)(2,1)} %q_ref.3, bf16[192,2048]{1,0:T(8,128)(2,1)} %k_ref.3, bf16[192,2048]{1,0:T(8,128)(2,1)} %v_ref.3), custom_call_target="tpu_custom_call" | custom-call | tf_op jit(solution)/shard_map/select/pallas_call | solution.py:244
  4.0 2.9 %collective-permute-start.3 = (bf16[3,640,128]{2,1,0:T(8,128)(2,1)}, bf16[3,640,128]{2,1,0:T(8,128)(2,1)S(1)}, u32[]{:S(2)}, u32[]{:S(2)}) collective-permute-start(bf16[3,640,128]{2,1,0:T(8,128)(2,1)} %get-tuple-element.21.own_ref), channel_id=1, source_target_pairs={{0,4},{4,0},{8,12},{12,8},{16,20},{20,16},{24,28},{28,24},{1,5},{5... | collective-permute-start | bytes 1474568 | tf_op jit(solution)/shard_map/ppermute | solution.py:182
  6.9 1.6 %collective-permute-start = (bf16[2,3,128,128]{3,2,1,0:T(8,128)(2,1)}, bf16[2,3,128,128]{3,2,1,0:T(8,128)(2,1)S(1)}, u32[]{:S(2)}, u32[]{:S(2)}) collective-permute-start(bf16[2,3,128,128]{3,2,1,0:T(8,128)(2,1)} %get-tuple-element.23.kv0), channel_id=1, source_target_pairs={{0,8},{4,12},{8,0},{12,4},{16,24},{20,28},{24,16},{28,20},{1,9},{5... | collective-permute-start | bytes 589832 | tf_op jit(solution)/shard_map/ppermute | solution.py:182
  8.5 2.6 %collective-permute-start.1 = (bf16[2,3,128,128]{3,2,1,0:T(8,128)(2,1)}, bf16[2,3,128,128]{3,2,1,0:T(8,128)(2,1)S(1)}, u32[]{:S(2)}, u32[]{:S(2)}) collective-permute-start(bf16[2,3,128,128]{3,2,1,0:T(8,128)(2,1)} %get-tuple-element.23.kv0), channel_id=1, source_target_pairs={{0,16},{4,20},{8,24},{12,28},{16,0},{20,4},{24,8},{28,12},{1,17},{... | collective-permute-start | bytes 589832 | tf_op jit(solution)/shard_map/ppermute | solution.py:182
  11.1 0.2 collective-permute-start.2
  11.3 11.1 %local.1.acc_in = f32[3,2048,128]{2,1,0:T(8,128)} custom-call(bf16[192,2048]{1,0:T(8,128)(2,1)} %q_ref.3, bf16[192,2048]{1,0:T(8,128)(2,1)} %k_ref.3, bf16[192,2048]{1,0:T(8,128)(2,1)} %v_ref.3), custom_call_target="tpu_custom_call" | custom-call | flops 3221225472 | bytes 12582912 | tf_op jit(solution)/shard_map/local/pallas_call | solution.py:262
  22.5 0.0 collective-permute-done.3.other_ref
  22.5 0.8 %copy-done.2 = bf16[3,640,128]{2,1,0:T(8,128)(2,1)} copy-done((bf16[3,640,128]{2,1,0:T(8,128)(2,1)}, bf16[3,640,128]{2,1,0:T(8,128)(2,1)S(1)}, u32[]{:S(2)}) %copy-start.2) | copy-done | bytes 491544
  23.3 6.5 %pair.1.acc_in = f32[3,2048,128]{2,1,0:T(8,128)} custom-call(s32[3,12]{1,0:T(4,128)} %off_ref.5, bf16[3,512,64]{2,1,0:T(8,128)(2,1)} %get-tuple-element.20.q_ref, bf16[3,640,128]{2,1,0:T(8,128)(2,1)} %get-tuple-element.21.own_ref, bf16[3,640,128]{2,1,0:T(8,128)(2,1)} %copy-done.2, f32[3,2048,128]{2,1,0:T(8,128)} %local.1.acc_in), custom_call_target="tpu_custom_call", output_to_operand_aliasing={{}: (4, {})} | custom-call | flops 805306368 | bytes 3145728 | tf_op jit(solution)/shard_map/pair/pallas_call | solution.py:273
  29.8 0.6 %copy-done.4 = bf16[2,3,128,128]{3,2,1,0:T(8,128)(2,1)} copy-done((bf16[2,3,128,128]{3,2,1,0:T(8,128)(2,1)}, bf16[2,3,128,128]{3,2,1,0:T(8,128)(2,1)S(1)}, u32[]{:S(2)}) %copy-start.4) | copy-done | bytes 196632
  30.5 0.1 copy-done.5
  30.5 0.7 %copy-done.6 = bf16[2,3,128,128]{3,2,1,0:T(8,128)(2,1)} copy-done((bf16[2,3,128,128]{3,2,1,0:T(8,128)(2,1)}, bf16[2,3,128,128]{3,2,1,0:T(8,128)(2,1)S(1)}, u32[]{:S(2)}) %copy-start.6) | copy-done | bytes 196632
  31.2 4.5 %far.1 = (f32[2,3,128,128]{3,2,1,0:T(8,128)}, bf16[3,256,128]{2,1,0:T(8,128)(2,1)}) custom-call(bf16[3,640,128]{2,1,0:T(8,128)(2,1)} %get-tuple-element.21.own_ref, bf16[3,640,128]{2,1,0:T(8,128)(2,1)} %copy-done.2, bf16[2,3,128,128]{3,2,1,0:T(8,128)(2,1)} %get-tuple-element.23.kv0, bf16[2,3,128,128]{3,2,1,0:T(8,128)(2,1)} %copy-done.4, ...), custom_call_target="tpu_custom_call" | custom-call | flops 402653184 | bytes 3145728 | tf_op jit(solution)/shard_map/far/pallas_call | solution.py:293
  35.7 0.3 collective-permute-start.4
  36.0 5.6 %collective-permute-done.4.got_ref = bf16[3,256,128]{2,1,0:T(8,128)(2,1)S(1)} collective-permute-done((bf16[3,256,128]{2,1,0:T(8,128)(2,1)}, bf16[3,256,128]{2,1,0:T(8,128)(2,1)S(1)}, u32[]{:S(2)}, u32[]{:S(2)}) %collective-permute-start.4) | collective-permute-done | bytes 196640 | tf_op jit(solution)/shard_map/ppermute | solution.py:182
  41.6 0.7 %copy-done.3 = bf16[3,256,128]{2,1,0:T(8,128)(2,1)} copy-done((bf16[3,256,128]{2,1,0:T(8,128)(2,1)}, bf16[3,256,128]{2,1,0:T(8,128)(2,1)S(1)}, u32[]{:S(2)}) %copy-start.3) | copy-done | bytes 196632
  42.3 5.5 %finish.1 = (bf16[192,512]{1,0:T(8,128)(2,1)}, bf16[192,512]{1,0:T(8,128)(2,1)}, bf16[192,512]{1,0:T(8,128)(2,1)}, bf16[192,512]{1,0:T(8,128)(2,1)}) custom-call(s32[3,12]{1,0:T(4,128)} %off_ref.5, f32[3,2048,128]{2,1,0:T(8,128)} %pair.1.acc_in, f32[2,3,128,128]{3,2,1,0:T(8,128)} %get-tuple-element.27.part_ref, bf16[3,256,128]{2,1,0:T(8,128)(2,1)} %copy-done.3), custom_call_target="tpu_custom_call" | custom-call | tf_op jit(solution)/shard_map/finish/pallas_call | solution.py:308
  47.8 0.0 collective-permute-start.5
  47.8 1.6 %collective-permute-start.6 = (bf16[192,512]{1,0:T(8,128)(2,1)}, bf16[192,512]{1,0:T(8,128)(2,1)S(1)}, u32[]{:S(2)}, u32[]{:S(2)}) collective-permute-start(bf16[192,512]{1,0:T(8,128)(2,1)} %get-tuple-element.31), channel_id=1, source_target_pairs={{0,2},{1,3},{2,0},{3,1},{4,6},{5,7},{6,4},{7,5},{8,10},{9,11},{10,... | collective-permute-start | bytes 589832 | tf_op jit(solution)/shard_map/ppermute | solution.py:182
  49.4 0.3 collective-permute-start.7
  49.7 6.1 %collective-permute-done.6.x2 = bf16[192,512]{1,0:T(8,128)(2,1)S(1)} collective-permute-done((bf16[192,512]{1,0:T(8,128)(2,1)}, bf16[192,512]{1,0:T(8,128)(2,1)S(1)}, u32[]{:S(2)}, u32[]{:S(2)}) %collective-permute-start.6) | collective-permute-done | bytes 196640 | tf_op jit(solution)/shard_map/ppermute | solution.py:182
  55.8 3.3 %collective-permute-done.7.x3 = bf16[192,512]{1,0:T(8,128)(2,1)S(1)} collective-permute-done((bf16[192,512]{1,0:T(8,128)(2,1)}, bf16[192,512]{1,0:T(8,128)(2,1)S(1)}, u32[]{:S(2)}, u32[]{:S(2)}) %collective-permute-start.7) | collective-permute-done | bytes 196640 | tf_op jit(solution)/shard_map/ppermute | solution.py:182
  59.1 0.9 %copy-done.1 = bf16[192,512]{1,0:T(8,128)(2,1)S(1)} copy-done((bf16[192,512]{1,0:T(8,128)(2,1)S(1)}, bf16[192,512]{1,0:T(8,128)(2,1)}, u32[]{:S(2)}) %copy-start.1) | copy-done | bytes 196632
  60.0 1.8 %project.1 = bf16[512,768]{1,0:T(8,128)(2,1)} custom-call(bf16[192,512]{1,0:T(8,128)(2,1)S(1)} %copy-done.1, bf16[192,512]{1,0:T(8,128)(2,1)S(1)} %collective-permute-done.5.x1, bf16[192,512]{1,0:T(8,128)(2,1)S(1)} %collective-permute-done.6.x2, bf16[192,512]{1,0:T(8,128)(2,1)S(1)} %collective-permute-done.7.x3, bf16[768,768]{1,0:T(8,128)(2,1)S(1)} %copy-done), custom_call_target="tpu_custom_call" | custom-call | tf_op jit(solution)/shard_map/project/pallas_call | solution.py:320
  (12 shorter events, 0.0 us)
Async XLA Ops:
  4.0 18.5 %collective-permute-start.3 = (bf16[3,640,128]{2,1,0:T(8,128)(2,1)}, bf16[3,640,128]{2,1,0:T(8,128)(2,1)S(1)}, u32[]{:S(2)}, u32[]{:S(2)}) collective-permute-start(bf16[3,640,128]{2,1,0:T(8,128)(2,1)} %get-tuple-element.21.own_ref), channel_id=1, source_target_pairs={{0,4},{4,0},{8,12},{12,8},{16,20},{20,16},{24,28},{28,24},{1,5},{5... | collective-permute-start | bytes 1474568 | tf_op jit(solution)/shard_map/ppermute | solution.py:182
  6.9 22.9 %collective-permute-start = (bf16[2,3,128,128]{3,2,1,0:T(8,128)(2,1)}, bf16[2,3,128,128]{3,2,1,0:T(8,128)(2,1)S(1)}, u32[]{:S(2)}, u32[]{:S(2)}) collective-permute-start(bf16[2,3,128,128]{3,2,1,0:T(8,128)(2,1)} %get-tuple-element.23.kv0), channel_id=1, source_target_pairs={{0,8},{4,12},{8,0},{12,4},{16,24},{20,28},{24,16},{28,20},{1,9},{5... | collective-permute-start | bytes 589832 | tf_op jit(solution)/shard_map/ppermute | solution.py:182
  8.5 21.3 %collective-permute-start.1 = (bf16[2,3,128,128]{3,2,1,0:T(8,128)(2,1)}, bf16[2,3,128,128]{3,2,1,0:T(8,128)(2,1)S(1)}, u32[]{:S(2)}, u32[]{:S(2)}) collective-permute-start(bf16[2,3,128,128]{3,2,1,0:T(8,128)(2,1)} %get-tuple-element.23.kv0), channel_id=1, source_target_pairs={{0,16},{4,20},{8,24},{12,28},{16,0},{20,4},{24,8},{28,12},{1,17},{... | collective-permute-start | bytes 589832 | tf_op jit(solution)/shard_map/ppermute | solution.py:182
  11.1 18.7 %collective-permute-start.2 = (bf16[2,3,128,128]{3,2,1,0:T(8,128)(2,1)}, bf16[2,3,128,128]{3,2,1,0:T(8,128)(2,1)S(1)}, u32[]{:S(2)}, u32[]{:S(2)}) collective-permute-start(bf16[2,3,128,128]{3,2,1,0:T(8,128)(2,1)} %get-tuple-element.23.kv0), channel_id=1, source_target_pairs={{0,24},{4,28},{8,16},{12,20},{16,8},{20,12},{24,0},{28,4},{1,25},{... | collective-permute-start | bytes 589832 | tf_op jit(solution)/shard_map/ppermute | solution.py:182
  22.5 0.8 %copy-start.2 = (bf16[3,640,128]{2,1,0:T(8,128)(2,1)}, bf16[3,640,128]{2,1,0:T(8,128)(2,1)S(1)}, u32[]{:S(2)}) copy-start(bf16[3,640,128]{2,1,0:T(8,128)(2,1)S(1)} %collective-permute-done.3.other_ref) | copy-start | bytes 1474564
  29.8 29.3 %copy-start = (bf16[768,768]{1,0:T(8,128)(2,1)S(1)}, bf16[768,768]{1,0:T(8,128)(2,1)}, u32[]{:S(2)}) copy-start(bf16[768,768]{1,0:T(8,128)(2,1)} %w_ref.1) | copy-start | bytes 3538948
  29.8 0.7 %copy-start.4 = (bf16[2,3,128,128]{3,2,1,0:T(8,128)(2,1)}, bf16[2,3,128,128]{3,2,1,0:T(8,128)(2,1)S(1)}, u32[]{:S(2)}) copy-start(bf16[2,3,128,128]{3,2,1,0:T(8,128)(2,1)S(1)} %collective-permute-done.kv1) | copy-start | bytes 589828
  29.8 0.7 %copy-start.5 = (bf16[2,3,128,128]{3,2,1,0:T(8,128)(2,1)}, bf16[2,3,128,128]{3,2,1,0:T(8,128)(2,1)S(1)}, u32[]{:S(2)}) copy-start(bf16[2,3,128,128]{3,2,1,0:T(8,128)(2,1)S(1)} %collective-permute-done.1.kv2) | copy-start | bytes 589828
  30.5 0.7 %copy-start.6 = (bf16[2,3,128,128]{3,2,1,0:T(8,128)(2,1)}, bf16[2,3,128,128]{3,2,1,0:T(8,128)(2,1)S(1)}, u32[]{:S(2)}) copy-start(bf16[2,3,128,128]{3,2,1,0:T(8,128)(2,1)S(1)} %collective-permute-done.2.kv3) | copy-start | bytes 589828
  35.7 5.9 %collective-permute-start.4 = (bf16[3,256,128]{2,1,0:T(8,128)(2,1)}, bf16[3,256,128]{2,1,0:T(8,128)(2,1)S(1)}, u32[]{:S(2)}, u32[]{:S(2)}) collective-permute-start(bf16[3,256,128]{2,1,0:T(8,128)(2,1)} %get-tuple-element.28), channel_id=1, source_target_pairs={{0,4},{4,0},{8,12},{12,8},{16,20},{20,16},{24,28},{28,24},{1,5},{5... | collective-permute-start | bytes 589832 | tf_op jit(solution)/shard_map/ppermute | solution.py:182
  41.6 0.7 %copy-start.3 = (bf16[3,256,128]{2,1,0:T(8,128)(2,1)}, bf16[3,256,128]{2,1,0:T(8,128)(2,1)S(1)}, u32[]{:S(2)}) copy-start(bf16[3,256,128]{2,1,0:T(8,128)(2,1)S(1)} %collective-permute-done.4.got_ref) | copy-start | bytes 589828
  47.8 1.9 %collective-permute-start.5 = (bf16[192,512]{1,0:T(8,128)(2,1)}, bf16[192,512]{1,0:T(8,128)(2,1)S(1)}, u32[]{:S(2)}, u32[]{:S(2)}) collective-permute-start(bf16[192,512]{1,0:T(8,128)(2,1)} %get-tuple-element.30), channel_id=1, source_target_pairs={{0,1},{1,0},{2,3},{3,2},{4,5},{5,4},{6,7},{7,6},{8,9},{9,8},{10,11... | collective-permute-start | bytes 589832 | tf_op jit(solution)/shard_map/ppermute | solution.py:182
  47.8 8.0 %collective-permute-start.6 = (bf16[192,512]{1,0:T(8,128)(2,1)}, bf16[192,512]{1,0:T(8,128)(2,1)S(1)}, u32[]{:S(2)}, u32[]{:S(2)}) collective-permute-start(bf16[192,512]{1,0:T(8,128)(2,1)} %get-tuple-element.31), channel_id=1, source_target_pairs={{0,2},{1,3},{2,0},{3,1},{4,6},{5,7},{6,4},{7,5},{8,10},{9,11},{10,... | collective-permute-start | bytes 589832 | tf_op jit(solution)/shard_map/ppermute | solution.py:182
  49.4 9.7 %collective-permute-start.7 = (bf16[192,512]{1,0:T(8,128)(2,1)}, bf16[192,512]{1,0:T(8,128)(2,1)S(1)}, u32[]{:S(2)}, u32[]{:S(2)}) collective-permute-start(bf16[192,512]{1,0:T(8,128)(2,1)} %get-tuple-element.32), channel_id=1, source_target_pairs={{0,3},{1,2},{2,1},{3,0},{4,7},{5,6},{6,5},{7,4},{8,11},{9,10},{10,... | collective-permute-start | bytes 589832 | tf_op jit(solution)/shard_map/ppermute | solution.py:182
  59.1 0.9 %copy-start.1 = (bf16[192,512]{1,0:T(8,128)(2,1)S(1)}, bf16[192,512]{1,0:T(8,128)(2,1)}, u32[]{:S(2)}) copy-start(bf16[192,512]{1,0:T(8,128)(2,1)} %get-tuple-element.29.x0) | copy-start | bytes 589828
